TPU v7x, 32 devices: a whole 2x2x4 slice. The times are simulated.
32 devices in a mesh: grp: 2 (over x), pts: 16 (over z, y, core).
Axes of the slice: x: 2, y: 2, z: 4, core: 2. Of those that a mesh axis runs over, the one named last changes fastest.
Arguments:
- support: bfloat16 [4096, 64], P(('grp', 'pts')), parts along dimension 0, may hold values from -9 to 9
- clouds: bfloat16 [8, 4096, 64], P(None, ('grp', 'pts')), parts along dimension 1, may hold values from -6 to 6
- member_weights: float32 [16], P('grp'), parts along dimension 0, may hold values from 1 to 10
Outputs:
- new_support: float32 [4096, 64], P(('grp', 'pts')), parts along dimension 0
There are 2 independent parts, one for each index of `grp`. A program takes and returns all parts, laid end to end along the dimension named above; each array names one. Nothing has to cross between parts.
All inputs are finite; a program needn't handle non-finite values.
Results may differ from a plain program's by a relative error of at most 0.001.
Values may be sent and summed in bfloat16 or wider, within the bound.
A program may use at most 128 MiB of HBM per device.

v0:
```python
import math

import jax
import jax.numpy as jnp
from jax import lax
from jax.sharding import PartitionSpec as P

ITERS = 3


EPS = 0.05


def combined_all(part, axis, combine):
    gathered = jax.tree.map(lambda a: lax.all_gather(a, axis), part)

    def take(source):
        return jax.tree.map(lambda a: lax.dynamic_index_in_dim(a, source, 0, False), gathered)

    return lax.fori_loop(
        1, lax.axis_size(axis), lambda source, state: combine(state, take(source)), take(0)
    )


def tile_cost(points, others):
    cross = lax.dot_general(
        points, others, (((1,), (1,)), ((), ())), preferred_element_type=jnp.float32
    )
    wide_a = points.astype(jnp.float32)
    wide_b = others.astype(jnp.float32)
    sq_a = jnp.sum(wide_a * wide_a, axis=1)
    sq_b = jnp.sum(wide_b * wide_b, axis=1)
    return (sq_a[:, None] + sq_b[None, :] - 2.0 * cross) / (2.0 * points.shape[1])


def join_stats(first, second):
    top = jnp.maximum(first[0], second[0])
    total = first[1] * jnp.exp(first[0] - top) + second[1] * jnp.exp(second[0] - top)
    return (top, total)


def merge_each(top, total):
    return combined_all((top, total), "pts", join_stats)


def per_device(support, clouds, member_weights):
    groups = lax.axis_size("pts")
    count_n = support.shape[0] * groups
    count_m = clouds.shape[1] * groups
    log_n = math.log(count_n)
    log_m = math.log(count_m)
    weights = member_weights / jnp.sum(member_weights)
    every_cloud = lax.all_gather(clouds, "pts", axis=1, tiled=True)

    def member_rows(packed):
        cloud, weight = packed
        cost = tile_cost(support, cloud)
        pot_g = jnp.zeros((cloud.shape[0],), jnp.float32)
        pot_f = jnp.zeros((support.shape[0],), jnp.float32)
        for step in range(ITERS):
            pot_f = -EPS * jax.nn.logsumexp((pot_g[None, :] - cost) / EPS, axis=1) - EPS * log_n
            scaled = (pot_f[:, None] - cost) / EPS
            top = jnp.max(scaled, axis=0)
            total = jnp.sum(jnp.exp(scaled - top[None, :]), axis=0)
            top, total = merge_each(top, total)
            pot_g = -EPS * (top + jnp.log(total)) - EPS * log_m
        plan = jnp.exp((pot_f[:, None] + pot_g[None, :] - cost) / EPS + log_n).astype(jnp.bfloat16)
        return weight * jnp.dot(plan, cloud, preferred_element_type=jnp.float32)

    terms = lax.map(member_rows, (every_cloud, weights))
    return jnp.sum(terms, axis=0)


def solution(mesh):
    in_specs = (P(("grp", "pts"), None), P(None, ("grp", "pts"), None), P("grp"))
    out_specs = P(("grp", "pts"), None)
    return jax.shard_map(
        per_device, mesh=mesh, in_specs=in_specs, out_specs=out_specs, check_vma=False
    )
```

profile of v0, /device:TPU:0, one launch (start us, length us, event | category | flops | bytes accessed | tf_op | source)
XLA Modules:
  0.0 1075.0 jit_solution(2546273230515968233)
XLA Ops:
  10.8 52.1 %all-gather.20.cloned.1.call-done = bf16[8,2048,64]{2,1,0:T(8,128)(2,1)} async-done(((bf16[8,128,64]{2,1,0:T(8,128)(2,1)}), bf16[8,2048,64]{2,1,0:T(8,128)(2,1)}) %all-gather.20.cloned.1.call-update) | async-done | bytes 2097168 | tf_op jit(solution)/shard_map/all_gather | solution.py:53
  62.9 1004.6 %while.132 = (s32[]{:T(128)}, f32[8,128,64]{1,2,0:T(8,128)S(1)}, f32[8]{0:T(128)S(1)}, bf16[128,64]{0,1:T(8,128)(2,1)}, bf16[8,2048,64]{2,1,0:T(8,128)(2,1)}, /*...) while((s32[]{:T(128)}, f32[8,128,64]{1,2,0:T(8,128)S(1)}, ...), condition=%wide.region_22.23_spmd, body=%wide.region_1.22_spmd.sunk | while | flops 80947344 | bytes 17984772 | solution.py:70
  67.8 19.2 %all-gather.13 = f32[32768]{0:T(1024)S(1)} all-gather(f32[2048]{0:T(1024)S(1)} %exponential_reduce_fusion.13), channel_id=3, replica_groups=mesh['grp'=2,'pts'=16] {'pts'}, dimensions={0}, use_global_device_ids=true | all-gather | bytes 139264 | tf_op jit(solution)/shard_map/while/body/eval_jaxpr/all_gather | solution.py:15
  107.8 19.1 %all-gather.15 = f32[32768]{0:T(1024)S(1)} all-gather(f32[2048]{0:T(1024)S(1)} %exponential_reduce_fusion.15), channel_id=5, replica_groups=mesh['grp'=2,'pts'=16] {'pts'}, dimensions={0}, use_global_device_ids=true | all-gather | bytes 139264 | tf_op jit(solution)/shard_map/while/body/eval_jaxpr/all_gather | solution.py:15
  147.6 19.1 %all-gather.17 = f32[32768]{0:T(1024)S(1)} all-gather(f32[2048]{0:T(1024)S(1)} %exponential_reduce_fusion.17), channel_id=7, replica_groups=mesh['grp'=2,'pts'=16] {'pts'}, dimensions={0}, use_global_device_ids=true | all-gather | bytes 139264 | tf_op jit(solution)/shard_map/while/body/eval_jaxpr/all_gather | solution.py:15
  193.5 19.1 %all-gather.13 = f32[32768]{0:T(1024)S(1)} all-gather(f32[2048]{0:T(1024)S(1)} %exponential_reduce_fusion.13), channel_id=3, replica_groups=mesh['grp'=2,'pts'=16] {'pts'}, dimensions={0}, use_global_device_ids=true | all-gather | bytes 139264 | tf_op jit(solution)/shard_map/while/body/eval_jaxpr/all_gather | solution.py:15
  233.3 19.1 %all-gather.15 = f32[32768]{0:T(1024)S(1)} all-gather(f32[2048]{0:T(1024)S(1)} %exponential_reduce_fusion.15), channel_id=5, replica_groups=mesh['grp'=2,'pts'=16] {'pts'}, dimensions={0}, use_global_device_ids=true | all-gather | bytes 139264 | tf_op jit(solution)/shard_map/while/body/eval_jaxpr/all_gather | solution.py:15
  273.3 19.0 %all-gather.17 = f32[32768]{0:T(1024)S(1)} all-gather(f32[2048]{0:T(1024)S(1)} %exponential_reduce_fusion.17), channel_id=7, replica_groups=mesh['grp'=2,'pts'=16] {'pts'}, dimensions={0}, use_global_device_ids=true | all-gather | bytes 139264 | tf_op jit(solution)/shard_map/while/body/eval_jaxpr/all_gather | solution.py:15
  319.2 19.0 %all-gather.13 = f32[32768]{0:T(1024)S(1)} all-gather(f32[2048]{0:T(1024)S(1)} %exponential_reduce_fusion.13), channel_id=3, replica_groups=mesh['grp'=2,'pts'=16] {'pts'}, dimensions={0}, use_global_device_ids=true | all-gather | bytes 139264 | tf_op jit(solution)/shard_map/while/body/eval_jaxpr/all_gather | solution.py:15
  359.0 19.0 %all-gather.15 = f32[32768]{0:T(1024)S(1)} all-gather(f32[2048]{0:T(1024)S(1)} %exponential_reduce_fusion.15), channel_id=5, replica_groups=mesh['grp'=2,'pts'=16] {'pts'}, dimensions={0}, use_global_device_ids=true | all-gather | bytes 139264 | tf_op jit(solution)/shard_map/while/body/eval_jaxpr/all_gather | solution.py:15
  398.8 19.0 %all-gather.17 = f32[32768]{0:T(1024)S(1)} all-gather(f32[2048]{0:T(1024)S(1)} %exponential_reduce_fusion.17), channel_id=7, replica_groups=mesh['grp'=2,'pts'=16] {'pts'}, dimensions={0}, use_global_device_ids=true | all-gather | bytes 139264 | tf_op jit(solution)/shard_map/while/body/eval_jaxpr/all_gather | solution.py:15
  444.7 19.0 %all-gather.13 = f32[32768]{0:T(1024)S(1)} all-gather(f32[2048]{0:T(1024)S(1)} %exponential_reduce_fusion.13), channel_id=3, replica_groups=mesh['grp'=2,'pts'=16] {'pts'}, dimensions={0}, use_global_device_ids=true | all-gather | bytes 139264 | tf_op jit(solution)/shard_map/while/body/eval_jaxpr/all_gather | solution.py:15
  484.6 19.0 %all-gather.15 = f32[32768]{0:T(1024)S(1)} all-gather(f32[2048]{0:T(1024)S(1)} %exponential_reduce_fusion.15), channel_id=5, replica_groups=mesh['grp'=2,'pts'=16] {'pts'}, dimensions={0}, use_global_device_ids=true | all-gather | bytes 139264 | tf_op jit(solution)/shard_map/while/body/eval_jaxpr/all_gather | solution.py:15
  524.4 19.0 %all-gather.17 = f32[32768]{0:T(1024)S(1)} all-gather(f32[2048]{0:T(1024)S(1)} %exponential_reduce_fusion.17), channel_id=7, replica_groups=mesh['grp'=2,'pts'=16] {'pts'}, dimensions={0}, use_global_device_ids=true | all-gather | bytes 139264 | tf_op jit(solution)/shard_map/while/body/eval_jaxpr/all_gather | solution.py:15
  570.3 19.0 %all-gather.13 = f32[32768]{0:T(1024)S(1)} all-gather(f32[2048]{0:T(1024)S(1)} %exponential_reduce_fusion.13), channel_id=3, replica_groups=mesh['grp'=2,'pts'=16] {'pts'}, dimensions={0}, use_global_device_ids=true | all-gather | bytes 139264 | tf_op jit(solution)/shard_map/while/body/eval_jaxpr/all_gather | solution.py:15
  610.1 19.0 %all-gather.15 = f32[32768]{0:T(1024)S(1)} all-gather(f32[2048]{0:T(1024)S(1)} %exponential_reduce_fusion.15), channel_id=5, replica_groups=mesh['grp'=2,'pts'=16] {'pts'}, dimensions={0}, use_global_device_ids=true | all-gather | bytes 139264 | tf_op jit(solution)/shard_map/while/body/eval_jaxpr/all_gather | solution.py:15
  649.9 19.0 %all-gather.17 = f32[32768]{0:T(1024)S(1)} all-gather(f32[2048]{0:T(1024)S(1)} %exponential_reduce_fusion.17), channel_id=7, replica_groups=mesh['grp'=2,'pts'=16] {'pts'}, dimensions={0}, use_global_device_ids=true | all-gather | bytes 139264 | tf_op jit(solution)/shard_map/while/body/eval_jaxpr/all_gather | solution.py:15
  695.8 19.0 %all-gather.13 = f32[32768]{0:T(1024)S(1)} all-gather(f32[2048]{0:T(1024)S(1)} %exponential_reduce_fusion.13), channel_id=3, replica_groups=mesh['grp'=2,'pts'=16] {'pts'}, dimensions={0}, use_global_device_ids=true | all-gather | bytes 139264 | tf_op jit(solution)/shard_map/while/body/eval_jaxpr/all_gather | solution.py:15
  735.7 19.0 %all-gather.15 = f32[32768]{0:T(1024)S(1)} all-gather(f32[2048]{0:T(1024)S(1)} %exponential_reduce_fusion.15), channel_id=5, replica_groups=mesh['grp'=2,'pts'=16] {'pts'}, dimensions={0}, use_global_device_ids=true | all-gather | bytes 139264 | tf_op jit(solution)/shard_map/while/body/eval_jaxpr/all_gather | solution.py:15
  775.5 19.0 %all-gather.17 = f32[32768]{0:T(1024)S(1)} all-gather(f32[2048]{0:T(1024)S(1)} %exponential_reduce_fusion.17), channel_id=7, replica_groups=mesh['grp'=2,'pts'=16] {'pts'}, dimensions={0}, use_global_device_ids=true | all-gather | bytes 139264 | tf_op jit(solution)/shard_map/while/body/eval_jaxpr/all_gather | solution.py:15
  821.4 19.0 %all-gather.13 = f32[32768]{0:T(1024)S(1)} all-gather(f32[2048]{0:T(1024)S(1)} %exponential_reduce_fusion.13), channel_id=3, replica_groups=mesh['grp'=2,'pts'=16] {'pts'}, dimensions={0}, use_global_device_ids=true | all-gather | bytes 139264 | tf_op jit(solution)/shard_map/while/body/eval_jaxpr/all_gather | solution.py:15
  840.4 18.0 %all-gather.12 = f32[32768]{0:T(1024)S(1)} all-gather(f32[2048]{0:T(1024)S(1)} %fusion.36), channel_id=2, replica_groups=mesh['grp'=2,'pts'=16] {'pts'}, dimensions={0}, use_global_device_ids=true | all-gather | bytes 139264 | tf_op jit(solution)/shard_map/while/body/eval_jaxpr/all_gather | solution.py:15
  861.2 19.0 %all-gather.15 = f32[32768]{0:T(1024)S(1)} all-gather(f32[2048]{0:T(1024)S(1)} %exponential_reduce_fusion.15), channel_id=5, replica_groups=mesh['grp'=2,'pts'=16] {'pts'}, dimensions={0}, use_global_device_ids=true | all-gather | bytes 139264 | tf_op jit(solution)/shard_map/while/body/eval_jaxpr/all_gather | solution.py:15
  880.2 18.0 %all-gather.14 = f32[32768]{0:T(1024)S(1)} all-gather(f32[2048]{0:T(1024)S(1)} %fusion.38), channel_id=4, replica_groups=mesh['grp'=2,'pts'=16] {'pts'}, dimensions={0}, use_global_device_ids=true | all-gather | bytes 139264 | tf_op jit(solution)/shard_map/while/body/eval_jaxpr/all_gather | solution.py:15
  901.0 19.0 %all-gather.17 = f32[32768]{0:T(1024)S(1)} all-gather(f32[2048]{0:T(1024)S(1)} %exponential_reduce_fusion.17), channel_id=7, replica_groups=mesh['grp'=2,'pts'=16] {'pts'}, dimensions={0}, use_global_device_ids=true | all-gather | bytes 139264 | tf_op jit(solution)/shard_map/while/body/eval_jaxpr/all_gather | solution.py:15
  920.0 18.0 %all-gather.16 = f32[32768]{0:T(1024)S(1)} all-gather(f32[2048]{0:T(1024)S(1)} %fusion.40), channel_id=6, replica_groups=mesh['grp'=2,'pts'=16] {'pts'}, dimensions={0}, use_global_device_ids=true | all-gather | bytes 139264 | tf_op jit(solution)/shard_map/while/body/eval_jaxpr/all_gather | solution.py:15
  946.9 19.0 %all-gather.13 = f32[32768]{0:T(1024)S(1)} all-gather(f32[2048]{0:T(1024)S(1)} %exponential_reduce_fusion.13), channel_id=3, replica_groups=mesh['grp'=2,'pts'=16] {'pts'}, dimensions={0}, use_global_device_ids=true | all-gather | bytes 139264 | tf_op jit(solution)/shard_map/while/body/eval_jaxpr/all_gather | solution.py:15
  965.9 18.0 %all-gather.12 = f32[32768]{0:T(1024)S(1)} all-gather(f32[2048]{0:T(1024)S(1)} %fusion.36), channel_id=2, replica_groups=mesh['grp'=2,'pts'=16] {'pts'}, dimensions={0}, use_global_device_ids=true | all-gather | bytes 139264 | tf_op jit(solution)/shard_map/while/body/eval_jaxpr/all_gather | solution.py:15
  986.7 19.0 %all-gather.15 = f32[32768]{0:T(1024)S(1)} all-gather(f32[2048]{0:T(1024)S(1)} %exponential_reduce_fusion.15), channel_id=5, replica_groups=mesh['grp'=2,'pts'=16] {'pts'}, dimensions={0}, use_global_device_ids=true | all-gather | bytes 139264 | tf_op jit(solution)/shard_map/while/body/eval_jaxpr/all_gather | solution.py:15
  1005.7 18.0 %all-gather.14 = f32[32768]{0:T(1024)S(1)} all-gather(f32[2048]{0:T(1024)S(1)} %fusion.38), channel_id=4, replica_groups=mesh['grp'=2,'pts'=16] {'pts'}, dimensions={0}, use_global_device_ids=true | all-gather | bytes 139264 | tf_op jit(solution)/shard_map/while/body/eval_jaxpr/all_gather | solution.py:15
  1026.6 19.0 %all-gather.17 = f32[32768]{0:T(1024)S(1)} all-gather(f32[2048]{0:T(1024)S(1)} %exponential_reduce_fusion.17), channel_id=7, replica_groups=mesh['grp'=2,'pts'=16] {'pts'}, dimensions={0}, use_global_device_ids=true | all-gather | bytes 139264 | tf_op jit(solution)/shard_map/while/body/eval_jaxpr/all_gather | solution.py:15
  1045.5 18.0 %all-gather.16 = f32[32768]{0:T(1024)S(1)} all-gather(f32[2048]{0:T(1024)S(1)} %fusion.40), channel_id=6, replica_groups=mesh['grp'=2,'pts'=16] {'pts'}, dimensions={0}, use_global_device_ids=true | all-gather | bytes 139264 | tf_op jit(solution)/shard_map/while/body/eval_jaxpr/all_gather | solution.py:15
  (1065 shorter events, 456.5 us)
Async XLA Ops:
  6.5 56.3 %all-gather.20.cloned.1.call-start = ((), (), s32[]{:S(2)}) async-start(), calls=%async_computation | async-start | bytes 4456448 | tf_op jit(solution)/shard_map/all_gather | solution.py:53
Sparse Core Ops, SparseCore 0:
  9.6 53.2 all-gather.19
where the time goes:
time: 1080 us; the launch traced here: 1070 us
  blocking collectives  886 us (82%)
  other arithmetic  64.1 us (6%)
  waiting for transfers between devices  52.1 us (5%)
  matrix products  30.2 us (3%)
  local copies, waits for them, and re-layouts  15.1 us (1%)
  loops' own time  13.9 us (1%)
  between operations  13.4 us (1%)
    all_gather x48, blocking collectives, combined_all(): gathered = jax.tree.map(lambda a: lax.all_gather(a, axis), part)  886 us
    all_gather x1, waiting for transfers between devices, per_device(): every_cloud = lax.all_gather(clouds, 'pts', axis=1, tiled=True)  52.1 us
  transfers between devices with their start and end apart: 1, of which 1 were waited for; matrix products, arithmetic and copies ran while one was open for 0% of the time, Pallas kernels for 0%

commit v1 on v0

v1 whole, which is shorter than its diff:
```python
import functools
import math

import jax
import jax.numpy as jnp
from jax import lax
from jax.experimental import pallas as pl
from jax.experimental.pallas import tpu as pltpu
from jax.sharding import PartitionSpec as P

ITERS = 3
EPS = 0.05
LANES = 128
GROUP = 32
EXTRA = 16
F32 = jnp.float32
BF16 = jnp.bfloat16


def split3(x):
    hi = x.astype(BF16).astype(F32)
    mid = (x - hi).astype(BF16).astype(F32)
    return hi, mid, (x - hi - mid).astype(BF16).astype(F32)


def kernel(
    dims, sup_ref, clouds_ref, weights_ref, out_ref,
    sup_send, cloud_send, sup_buf, cloud_buf, left, right, mat, top, u_ref, part,
    col, stat_send, stat_recv, plan, out_send, out_recv,
    sup_ssem, sup_rsem, cl_ssem, cl_rsem, relay_ssem, relay_rsem,
    stat_ssem, stat_rsem, out_ssem, out_rsem,
):
    memb, sib, shard, dim = dims
    devices = memb * sib
    rows = memb * shard
    cols = devices * shard
    chunk = 2048 if cols % 2048 == 0 else cols
    alpha = math.log2(math.e) / (EPS * 2.0 * dim)
    me = lax.axis_index("pts")
    mine = me // sib
    r = lax.rem(me, sib)

    def peer(d):
        return lax.rem(mine + d, memb)

    def at(cloud, place):
        return {"pts": cloud * sib + place}

    barrier = pltpu.get_barrier_semaphore()
    for d in range(1, memb):
        pl.semaphore_signal(barrier, inc=1, device_id=at(peer(d), r))
    for s in range(1, sib):
        pl.semaphore_signal(barrier, inc=1, device_id=at(mine, lax.rem(r + s, sib)))

    sup_send[...] = jnp.transpose(sup_ref[...].astype(F32)).astype(BF16)
    for k in range(memb):
        cloud_send[k] = jnp.transpose(clouds_ref[k].astype(F32)).astype(BF16)
    sup_buf[mine] = sup_send[...]
    cloud_buf[me] = cloud_send[mine]
    pl.semaphore_wait(barrier, memb - 1 + sib - 1)

    def cloud_copy(d):
        target = peer(d)
        return pltpu.make_async_remote_copy(
            cloud_send.at[target], cloud_buf.at[me], cl_ssem.at[d], cl_rsem.at[d],
            device_id=at(target, r), device_id_type=pl.DeviceIdType.MESH)

    def sup_copy(d):
        return pltpu.make_async_remote_copy(
            sup_send, sup_buf.at[mine], sup_ssem.at[d], sup_rsem.at[d],
            device_id=at(peer(d), r), device_id_type=pl.DeviceIdType.MESH)

    def relay_copy(d, s):
        owner = lax.rem(mine + memb - d, memb) * sib + r
        return pltpu.make_async_remote_copy(
            cloud_buf.at[owner], cloud_buf.at[owner], relay_ssem.at[d, s], relay_rsem.at[d, s],
            device_id=at(mine, lax.rem(r + s, sib)), device_id_type=pl.DeviceIdType.MESH)

    order = [memb // 2]
    for d in range(1, memb):
        if d not in order:
            order.append(d)
    for d in order:
        cloud_copy(d).start()
    for d in order:
        sup_copy(d).start()
    for s in range(1, sib):
        relay_copy(0, s).start()
    for d in range(1, memb):
        cloud_copy(d).wait_recv()
        for s in range(1, sib):
            relay_copy(d, s).start()

    ones3 = jnp.ones((3, shard), F32)
    zeros = jnp.zeros((EXTRA - 6, shard), F32)

    def make_left(c, _):
        x = sup_buf[c].astype(F32)
        norm = split3(-jnp.sum(x * x, axis=0, keepdims=True))
        block = jnp.concatenate([2.0 * x, ones3, *norm, zeros], axis=0)
        left[pl.ds(pl.multiple_of(c * shard, shard), shard), :] = jnp.transpose(block).astype(BF16)
        return 0

    def make_right(q, _):
        x = cloud_buf[q].astype(F32)
        norm = split3(-jnp.sum(x * x, axis=0, keepdims=True))
        block = jnp.concatenate([x, *norm, ones3, zeros], axis=0)
        right[:, pl.ds(pl.multiple_of(q * shard, shard), shard)] = block.astype(BF16)
        return 0

    for d in range(1, memb):
        sup_copy(d).wait_recv()
    lax.fori_loop(0, memb, make_left, 0)
    for d in range(memb):
        for s in range(1, sib):
            relay_copy(d, s).wait_recv()
    lax.fori_loop(0, devices, make_right, 0)

    wide = 256
    def cost_step(j, _):
        span = pl.ds(pl.multiple_of(j * wide, wide), wide)
        w = right[:, span]
        for i in range(0, rows, 256):
            h = slice(i, i + 256)
            t = jnp.dot(left[h, :], w, preferred_element_type=F32)
            mat[h, span] = t
            top[h, :] = jnp.maximum(top[h, :], jnp.maximum(t[:, :LANES], t[:, LANES:]))
        return 0

    top[...] = jnp.full(top.shape, -3e38, F32)
    lax.fori_loop(0, cols // wide, cost_step, 0)
    top[...] = jnp.broadcast_to(jnp.max(top[...], axis=1, keepdims=True), top.shape)

    tiles = chunk // LANES
    groups = rows // GROUP

    def tile(g, base, c):
        return (
            pl.ds(pl.multiple_of(g * GROUP, GROUP), GROUP),
            pl.ds(pl.multiple_of(base + c * LANES, LANES), LANES),
        )

    def rows_of(ref, g):
        return ref[pl.ds(pl.multiple_of(g * GROUP, GROUP), GROUP), :]

    def fold(x, op):
        acc = x[0:8]
        for i in range(8, GROUP, 8):
            acc = op(acc, x[i:i + 8])
        return acc

    def lanes(ref, base, c):
        return ref[:, base + c * LANES:base + (c + 1) * LANES]

    for base in range(0, cols, chunk):
        def max_step(g, best, base=base):
            a = rows_of(top, g)
            return tuple(
                jnp.maximum(best[c], fold(mat[tile(g, base, c)] - a, jnp.maximum))
                for c in range(tiles))

        start = tuple(jnp.full((8, LANES), -3e38, F32) for _ in range(tiles))
        best = lax.fori_loop(0, groups, max_step, start)
        for c in range(tiles):
            b = jnp.max(best[c], axis=0, keepdims=True)
            stat_send[0, :, base + c * LANES:base + (c + 1) * LANES] = b
            col[0, :, base + c * LANES:base + (c + 1) * LANES] = jnp.broadcast_to(b, (8, LANES))
            col[1, :, base + c * LANES:base + (c + 1) * LANES] = jnp.broadcast_to(
                jnp.exp2(b * alpha), (8, LANES))

    def stat_copy(step, s):
        n = 2 if step == 0 else 1
        lo = 0 if step == 0 else 1 + step
        return pltpu.make_async_remote_copy(
            stat_send.at[pl.ds(lo, n)], stat_recv.at[s, pl.ds(lo, n)],
            stat_ssem.at[step, s], stat_rsem.at[step, s],
            device_id=at(mine, lax.rem(r + s, sib)), device_id_type=pl.DeviceIdType.MESH)

    def times(x, y):
        return x * jnp.concatenate([y] * (GROUP // 8), axis=0)

    for step in range(ITERS):
        for base in range(0, cols, chunk):
            def row_step(g, _, base=base):
                acc = jnp.zeros((GROUP, LANES), F32)
                a = rows_of(top, g)
                for c in range(tiles):
                    k = mat[tile(g, base, c)]
                    if step == 0:
                        b = jnp.concatenate([lanes(col.at[0], base, c)] * (GROUP // 8), axis=0)
                        k = jnp.exp2(((k - a) - b) * alpha)
                        mat[tile(g, base, c)] = k
                    acc = acc + times(k, lanes(col.at[1], base, c))
                if base > 0:
                    acc = acc + rows_of(part, g)
                part[pl.ds(pl.multiple_of(g * GROUP, GROUP), GROUP), :] = acc
                return 0

            lax.fori_loop(0, groups, row_step, 0)
        total = jnp.sum(part[...], axis=1, keepdims=True)
        u_ref[...] = jnp.broadcast_to(1.0 / (total * rows_all(dims)), u_ref.shape)
        for base in range(0, cols, chunk):
            def col_step(g, acc, base=base):
                u = rows_of(u_ref, g)
                return tuple(
                    acc[c] + fold(mat[tile(g, base, c)] * u, jnp.add) for c in range(tiles))

            start = tuple(jnp.zeros((8, LANES), F32) for _ in range(tiles))
            acc = lax.fori_loop(0, groups, col_step, start)
            for c in range(tiles):
                stat_send[1 + step, :, base + c * LANES:base + (c + 1) * LANES] = jnp.sum(
                    acc[c], axis=0, keepdims=True)
        for s in range(1, sib):
            stat_copy(step, s).start()
        for s in range(1, sib):
            stat_copy(step, s).wait_recv()
        high = stat_send[0]
        for s in range(1, sib):
            high = jnp.maximum(high, stat_recv[s, 0])
        local = jnp.exp2((stat_send[0] - high) * alpha)
        total = local * stat_send[1 + step]
        for s in range(1, sib):
            total = total + jnp.exp2((stat_recv[s, 0] - high) * alpha) * stat_recv[s, 1 + step]
        v = local / (total * float(cols))
        col[1] = jnp.broadcast_to(v, (8, cols))

    weight_sum = weights_ref[0]
    for k in range(1, memb):
        weight_sum = weight_sum + weights_ref[k]
    weight = weights_ref[mine] / weight_sum

    def out_copy(d):
        target = peer(d)
        return pltpu.make_async_remote_copy(
            out_send.at[target], out_recv.at[mine], out_ssem.at[d], out_rsem.at[d],
            device_id=at(target, r), device_id_type=pl.DeviceIdType.MESH)

    for d in order + [0]:
        block = peer(d)

        def plan_step(g, _):
            u = rows_of(u_ref, block * (shard // GROUP) + g) * rows_all(dims)
            for base in range(0, cols, chunk):
                for c in range(tiles):
                    p = times(mat[tile(block * (shard // GROUP) + g, base, c)] * u,
                              lanes(col.at[1], base, c))
                    plan[pl.ds(pl.multiple_of(g * GROUP, GROUP), GROUP),
                         base + c * LANES:base + (c + 1) * LANES] = p.astype(BF16)
            return 0

        lax.fori_loop(0, shard // GROUP, plan_step, 0)
        term = lax.dot_general(
            plan[...], right[:dim, :], (((1,), (1,)), ((), ())), preferred_element_type=F32)
        term = jnp.transpose(term * weight)
        if d == 0:
            out_recv[mine] = term
        else:
            out_send[block] = term
            out_copy(d).start()

    for d in range(1, memb):
        out_copy(d).wait_recv()
    total = out_recv[0]
    for k in range(1, memb):
        total = total + out_recv[k]
    out_ref[...] = jnp.transpose(total)

    for d in range(1, memb):
        cloud_copy(d).wait_send()
        sup_copy(d).wait_send()
        out_copy(d).wait_send()
    for s in range(1, sib):
        for d in range(memb):
            relay_copy(d, s).wait_send()
        for step in range(ITERS):
            stat_copy(step, s).wait_send()


def rows_all(dims):
    memb, sib, shard, _ = dims
    return float(memb * sib * shard)


def per_device(support, clouds, member_weights):
    devices = lax.axis_size("pts")
    memb, shard, dim = clouds.shape
    sib = devices // memb
    rows, cols = memb * shard, devices * shard
    dims = (memb, sib, shard, dim)
    vmem, dma = pltpu.VMEM, pltpu.SemaphoreType.DMA
    return pl.pallas_call(
        functools.partial(kernel, dims),
        out_shape=jax.ShapeDtypeStruct((shard, dim), F32),
        in_specs=[
            pl.BlockSpec(memory_space=pltpu.VMEM),
            pl.BlockSpec(memory_space=pltpu.VMEM),
            pl.BlockSpec(memory_space=pltpu.SMEM),
        ],
        out_specs=pl.BlockSpec(memory_space=pltpu.VMEM),
        scratch_shapes=[
            vmem((dim, shard), BF16),
            vmem((memb, dim, shard), BF16),
            vmem((memb, dim, shard), BF16),
            vmem((devices, dim, shard), BF16),
            vmem((rows, dim + EXTRA), BF16),
            vmem((dim + EXTRA, cols), BF16),
            vmem((rows, cols), F32),
            vmem((rows, LANES), F32),
            vmem((rows, LANES), F32),
            vmem((rows, LANES), F32),
            vmem((2, 8, cols), F32),
            vmem((1 + ITERS, 1, cols), F32),
            vmem((sib, 1 + ITERS, 1, cols), F32),
            vmem((shard, cols), BF16),
            vmem((memb, dim, shard), F32),
            vmem((memb, dim, shard), F32),
            dma((memb,)), dma((memb,)),
            dma((memb,)), dma((memb,)),
            dma((memb, sib)), dma((memb, sib)),
            dma((ITERS, sib)), dma((ITERS, sib)),
            dma((memb,)), dma((memb,)),
        ],
        compiler_params=pltpu.CompilerParams(
            collective_id=0, has_side_effects=True,
            vmem_limit_bytes=rows * cols * 4 + (16 << 20)),
    )(support, clouds, member_weights)


def solution(mesh):
    in_specs = (P(("grp", "pts"), None), P(None, ("grp", "pts"), None), P("grp"))
    out_specs = P(("grp", "pts"), None)
    return jax.shard_map(
        per_device, mesh=mesh, in_specs=in_specs, out_specs=out_specs, check_vma=False
    )
```

time: 1080 us -> 39.5 us (0.04)
  blocking collectives: 886 us -> 0 us
  other arithmetic: 64.1 us -> 0 us
  waiting for transfers between devices: 52.1 us -> 0 us
  Pallas kernels: 0 us -> 36.6 us
  matrix products: 30.2 us -> 0 us
  loops' own time: 13.9 us -> 0 us
  between operations: 13.4 us -> 0.03 us
  local copies, waits for them, and re-layouts: 15.1 us -> 2.61 us
    all_gather x48 -> x0, blocking collectives: 886 us -> none  [combined_all(): gathered = jax.tree.map(lambda a: lax.all_gather(a, axis), part)]
    all_gather x1 -> x0, waiting for transfers between devices: 52.1 us -> none  [per_device(): every_cloud = lax.all_gather(clouds, 'pts', axis=1, tiled=True)]
    reduce_sum x66 -> x0, other arithmetic: 43.2 us -> none  [the longest x24 16 us: member_rows(): total = jnp.sum(jnp.exp(scaled - top[None, :]), axis=0)]
    pallas_call x0 -> x1, Pallas kernels: none -> 36.6 us  [per_device(): pl.pallas_call(functools.partial(kernel, dims), out_shape=jax.ShapeDtypeS...]
    dot_general x16 -> x0, matrix products: 30.2 us -> none  [the longest x8 18.4 us: member_rows(): return weight * jnp.dot(plan, cloud, preferred_element_type=jnp.float32)]
    reduce_max x40 -> x0, other arithmetic: 14.1 us -> none  [the longest x24 8.54 us: member_rows(): top = jnp.max(scaled, axis=0)]
    another operation x25 -> x0, loops' own time: 13.9 us -> none  [the longest x24 12.4 us: combined_all(): lax.fori_loop(1, lax.axis_size(axis), lambda source, state: combine(state...]
    dynamic_slice x416 -> x0, local copies, waits for them, and re-layouts: 12.1 us -> none  [the longest x408 7.33 us: take(): lax.dynamic_index_in_dim(a, source, 0, False)]
  transfers between devices with their start and end apart: 1 -> 0, of which waited for: 1 -> 0; matrix products, arithmetic and copies ran while one was open for 0% -> 0% of each run, Pallas kernels for 0% -> 0%
where the time goes in v1:
time: 39.5 us; the launch traced here: 39.3 us
  Pallas kernels  36.6 us (93%)
  local copies, waits for them, and re-layouts  2.61 us (7%)
    pallas_call x1, Pallas kernels, per_device(): pl.pallas_call(functools.partial(kernel, dims), out_shape=jax.ShapeDtypeS...  36.6 us
    unnamed x4, local copies, waits for them, and re-layouts  1.92 us

profile of v1, /device:TPU:0, one launch (start us, length us, event | category | flops | bytes accessed | tf_op | source)
XLA Modules:
  0.0 39.3 jit_solution(1293488136622636261)
XLA Ops:
  0.0 0.8 %copy.4.sup_ref = bf16[128,64]{1,0:T(8,128)(2,1)S(1)} copy(bf16[128,64]{0,1:T(8,128)(2,1)} %param.3) | data formatting | bytes 32768 | tf_op args[0]
  0.8 0.0 copy-start
  0.8 1.1 %copy.5.clouds_ref = bf16[8,128,64]{2,1,0:T(8,128)(2,1)S(1)} copy(bf16[8,128,64]{1,2,0:T(8,128)(2,1)} %param.4) | data formatting | bytes 262144 | tf_op args[1]
  1.9 0.0 copy-done
  1.9 36.6 %shard_map.37 = f32[128,64]{1,0:T(8,128)S(1)} custom-call(bf16[128,64]{1,0:T(8,128)(2,1)S(1)} %copy.4.sup_ref, bf16[8,128,64]{2,1,0:T(8,128)(2,1)S(1)} %copy.5.clouds_ref, f32[8]{0:T(128)S(1)} %copy-done), custom_call_target="tpu_custom_call" | custom-call | tf_op jit(solution)/shard_map/pallas_call | solution.py:291
  38.6 0.7 %copy.6 = f32[128,64]{0,1:T(8,128)} copy(f32[128,64]{1,0:T(8,128)S(1)} %shard_map.37) | data formatting | bytes 65536 | tf_op jit(solution)/shard_map/pallas_call | solution.py:291
Async XLA Ops:
  0.8 1.1 %copy-start = (f32[8]{0:T(128)S(1)}, f32[8]{0:T(128)}, u32[]{:S(2)}) copy-start(f32[8]{0:T(128)} %weights_ref.1) | copy-start | bytes 100

commit v2 on v1

--- a/solution.py
+++ b/solution.py
@@ -25,10 +25,10 @@
 
 def kernel(
     dims, sup_ref, clouds_ref, weights_ref, out_ref,
-    sup_send, cloud_send, sup_buf, cloud_buf, left, right, mat, top, u_ref, part,
-    col, stat_send, stat_recv, plan, out_send, out_recv,
-    sup_ssem, sup_rsem, cl_ssem, cl_rsem, relay_ssem, relay_rsem,
-    stat_ssem, stat_rsem, out_ssem, out_rsem,
+    sup_buf, cloud_buf, left, right, mat, top, u_ref, part,
+    col, stat_send, stat_recv, plan, out_send, pair_recv, out_recv,
+    sup_ssem, sup_rsem, pass_ssem, pass_rsem, cl_ssem, cl_rsem, relay_ssem, relay_rsem,
+    stat_ssem, stat_rsem, pair_ssem, pair_rsem, out_ssem, out_rsem, own_sem,
 ):
     memb, sib, shard, dim = dims
     devices = memb * sib
@@ -39,6 +39,9 @@
     me = lax.axis_index("pts")
     mine = me // sib
     r = lax.rem(me, sib)
+    outer = memb // 2
+    line, side = mine // 2, lax.rem(mine, 2)
+    twin = line * 2 + 1 - side
 
     def peer(d):
         return lax.rem(mine + d, memb)
@@ -52,23 +55,29 @@
     for s in range(1, sib):
         pl.semaphore_signal(barrier, inc=1, device_id=at(mine, lax.rem(r + s, sib)))
 
-    sup_send[...] = jnp.transpose(sup_ref[...].astype(F32)).astype(BF16)
-    for k in range(memb):
-        cloud_send[k] = jnp.transpose(clouds_ref[k].astype(F32)).astype(BF16)
-    sup_buf[mine] = sup_send[...]
-    cloud_buf[me] = cloud_send[mine]
+    own_sup = pltpu.make_async_copy(sup_ref, sup_buf.at[mine], own_sem.at[0])
+    own_cloud = pltpu.make_async_copy(clouds_ref.at[mine], cloud_buf.at[me], own_sem.at[1])
+    own_sup.start()
+    own_cloud.start()
     pl.semaphore_wait(barrier, memb - 1 + sib - 1)
 
     def cloud_copy(d):
         target = peer(d)
         return pltpu.make_async_remote_copy(
-            cloud_send.at[target], cloud_buf.at[me], cl_ssem.at[d], cl_rsem.at[d],
+            clouds_ref.at[target], cloud_buf.at[me], cl_ssem.at[d], cl_rsem.at[d],
             device_id=at(target, r), device_id_type=pl.DeviceIdType.MESH)
 
-    def sup_copy(d):
-        return pltpu.make_async_remote_copy(
-            sup_send, sup_buf.at[mine], sup_ssem.at[d], sup_rsem.at[d],
-            device_id=at(peer(d), r), device_id_type=pl.DeviceIdType.MESH)
+    def sup_copy(e):
+        target = lax.rem(line + e, outer) * 2 + side
+        return pltpu.make_async_remote_copy(
+            sup_ref, sup_buf.at[mine], sup_ssem.at[e], sup_rsem.at[e],
+            device_id=at(target, r), device_id_type=pl.DeviceIdType.MESH)
+
+    def pass_copy(e):
+        owner = lax.rem(line + outer - e, outer) * 2 + side
+        return pltpu.make_async_remote_copy(
+            sup_buf.at[owner], sup_buf.at[owner], pass_ssem.at[e], pass_rsem.at[e],
+            device_id=at(twin, r), device_id_type=pl.DeviceIdType.MESH)
 
     def relay_copy(d, s):
         owner = lax.rem(mine + memb - d, memb) * sib + r
@@ -76,20 +85,28 @@
             cloud_buf.at[owner], cloud_buf.at[owner], relay_ssem.at[d, s], relay_rsem.at[d, s],
             device_id=at(mine, lax.rem(r + s, sib)), device_id_type=pl.DeviceIdType.MESH)
 
-    order = [memb // 2]
-    for d in range(1, memb):
-        if d not in order:
-            order.append(d)
-    for d in order:
-        cloud_copy(d).start()
-    for d in order:
-        sup_copy(d).start()
+    def dist(i):
+        j = lax.rem(i + memb - 1, memb) + 1
+        return memb // 2 + (j // 2) * (2 * lax.rem(j, 2) - 1)
+
+    for e in range(1, outer):
+        sup_copy(e).start()
+
+    def send_step(i, _):
+        cloud_copy(dist(i)).start()
+        return 0
+
+    lax.fori_loop(1, memb, send_step, 0)
+    own_sup.wait()
+    pass_copy(0).start()
+    own_cloud.wait()
     for s in range(1, sib):
         relay_copy(0, s).start()
-    for d in range(1, memb):
-        cloud_copy(d).wait_recv()
-        for s in range(1, sib):
-            relay_copy(d, s).start()
+    for e in range(1, outer):
+        sup_copy(e).wait_recv()
+        pass_copy(e).start()
+    for e in range(outer):
+        pass_copy(e).wait_recv()
 
     ones3 = jnp.ones((3, shard), F32)
     zeros = jnp.zeros((EXTRA - 6, shard), F32)
@@ -108,27 +125,41 @@
         right[:, pl.ds(pl.multiple_of(q * shard, shard), shard)] = block.astype(BF16)
         return 0
 
-    for d in range(1, memb):
-        sup_copy(d).wait_recv()
     lax.fori_loop(0, memb, make_left, 0)
-    for d in range(memb):
+
+    block_cols = sib * shard
+    wide = 256 if block_cols % 256 == 0 else LANES
+    top[...] = jnp.full(top.shape, -3e38, F32)
+
+    def arrive_step(i, _):
+        @pl.when(i < memb - 1)
+        def _():
+            cloud_copy(dist(i + 1)).wait_recv()
+            for s in range(1, sib):
+                relay_copy(dist(i + 1), s).start()
+
+        d = dist(i)
         for s in range(1, sib):
             relay_copy(d, s).wait_recv()
-    lax.fori_loop(0, devices, make_right, 0)
-
-    wide = 256
-    def cost_step(j, _):
-        span = pl.ds(pl.multiple_of(j * wide, wide), wide)
-        w = right[:, span]
-        for i in range(0, rows, 256):
-            h = slice(i, i + 256)
-            t = jnp.dot(left[h, :], w, preferred_element_type=F32)
-            mat[h, span] = t
-            top[h, :] = jnp.maximum(top[h, :], jnp.maximum(t[:, :LANES], t[:, LANES:]))
-        return 0
-
-    top[...] = jnp.full(top.shape, -3e38, F32)
-    lax.fori_loop(0, cols // wide, cost_step, 0)
+        owner = lax.rem(mine + memb - d, memb)
+        lax.fori_loop(0, sib, lambda q, _: make_right(owner * sib + q, 0), 0)
+
+        def cost_step(j, _):
+            span = pl.ds(pl.multiple_of(owner * block_cols + j * wide, wide), wide)
+            w = right[:, span]
+            for h in range(0, rows, 256):
+                t = jnp.dot(left[h:h + 256, :], w, preferred_element_type=F32)
+                mat[h:h + 256, span] = t
+                most = t[:, :LANES]
+                for n in range(LANES, wide, LANES):
+                    most = jnp.maximum(most, t[:, n:n + LANES])
+                top[h:h + 256, :] = jnp.maximum(top[h:h + 256, :], most)
+            return 0
+
+        lax.fori_loop(0, block_cols // wide, cost_step, 0)
+        return 0
+
+    lax.fori_loop(0, memb, arrive_step, 0)
     top[...] = jnp.broadcast_to(jnp.max(top[...], axis=1, keepdims=True), top.shape)
 
     tiles = chunk // LANES
@@ -229,14 +260,24 @@
         weight_sum = weight_sum + weights_ref[k]
     weight = weights_ref[mine] / weight_sum
 
-    def out_copy(d):
-        target = peer(d)
-        return pltpu.make_async_remote_copy(
-            out_send.at[target], out_recv.at[mine], out_ssem.at[d], out_rsem.at[d],
+    def pair_copy(e):
+        target = lax.rem(line + e, outer)
+        return pltpu.make_async_remote_copy(
+            out_send.at[target * 2 + 1 - side], pair_recv.at[target],
+            pair_ssem.at[e], pair_rsem.at[e],
+            device_id=at(twin, r), device_id_type=pl.DeviceIdType.MESH)
+
+    def out_copy(e):
+        target = lax.rem(line + e, outer) * 2 + side
+        return pltpu.make_async_remote_copy(
+            out_send.at[target], out_recv.at[e], out_ssem.at[e], out_rsem.at[e],
             device_id=at(target, r), device_id_type=pl.DeviceIdType.MESH)
 
-    for d in order + [0]:
-        block = peer(d)
+    def send_block(i, _):
+        second = i // outer
+        e = outer - 1 - lax.rem(i, outer)
+        target = lax.rem(line + e, outer)
+        block = target * 2 + lax.rem(side + 1 + second, 2)
 
         def plan_step(g, _):
             u = rows_of(u_ref, block * (shard // GROUP) + g) * rows_all(dims)
@@ -252,23 +293,38 @@
         term = lax.dot_general(
             plan[...], right[:dim, :], (((1,), (1,)), ((), ())), preferred_element_type=F32)
         term = jnp.transpose(term * weight)
-        if d == 0:
-            out_recv[mine] = term
-        else:
+
+        @pl.when(second == 0)
+        def _():
             out_send[block] = term
-            out_copy(d).start()
-
-    for d in range(1, memb):
-        out_copy(d).wait_recv()
-    total = out_recv[0]
-    for k in range(1, memb):
-        total = total + out_recv[k]
-    out_ref[...] = jnp.transpose(total)
+            pair_copy(e).start()
+
+        @pl.when(second == 1)
+        def _():
+            pair_copy(e).wait_recv()
+            out_send[block] = term + pair_recv[target]
+
+            @pl.when(e > 0)
+            def _():
+                out_copy(e).start()
+
+        return 0
+
+    lax.fori_loop(0, memb, send_block, 0)
+    total = out_send[mine]
+    for e in range(1, outer):
+        out_copy(e).wait_recv()
+        total = total + out_recv[e]
+    out_ref[...] = total
 
     for d in range(1, memb):
         cloud_copy(d).wait_send()
-        sup_copy(d).wait_send()
-        out_copy(d).wait_send()
+    for e in range(outer):
+        pass_copy(e).wait_send()
+        pair_copy(e).wait_send()
+        if e > 0:
+            sup_copy(e).wait_send()
+            out_copy(e).wait_send()
     for s in range(1, sib):
         for d in range(memb):
             relay_copy(d, s).wait_send()
@@ -288,18 +344,16 @@
     rows, cols = memb * shard, devices * shard
     dims = (memb, sib, shard, dim)
     vmem, dma = pltpu.VMEM, pltpu.SemaphoreType.DMA
-    return pl.pallas_call(
+    out = pl.pallas_call(
         functools.partial(kernel, dims),
-        out_shape=jax.ShapeDtypeStruct((shard, dim), F32),
+        out_shape=jax.ShapeDtypeStruct((dim, shard), F32),
         in_specs=[
-            pl.BlockSpec(memory_space=pltpu.VMEM),
-            pl.BlockSpec(memory_space=pltpu.VMEM),
+            pl.BlockSpec(memory_space=pl.ANY),
+            pl.BlockSpec(memory_space=pl.ANY),
             pl.BlockSpec(memory_space=pltpu.SMEM),
         ],
         out_specs=pl.BlockSpec(memory_space=pltpu.VMEM),
         scratch_shapes=[
-            vmem((dim, shard), BF16),
-            vmem((memb, dim, shard), BF16),
             vmem((memb, dim, shard), BF16),
             vmem((devices, dim, shard), BF16),
             vmem((rows, dim + EXTRA), BF16),
@@ -313,17 +367,21 @@
             vmem((sib, 1 + ITERS, 1, cols), F32),
             vmem((shard, cols), BF16),
             vmem((memb, dim, shard), F32),
-            vmem((memb, dim, shard), F32),
-            dma((memb,)), dma((memb,)),
+            vmem((memb // 2, dim, shard), F32),
+            vmem((memb // 2, dim, shard), F32),
+            dma((memb // 2,)), dma((memb // 2,)),
+            dma((memb // 2,)), dma((memb // 2,)),
             dma((memb,)), dma((memb,)),
             dma((memb, sib)), dma((memb, sib)),
             dma((ITERS, sib)), dma((ITERS, sib)),
-            dma((memb,)), dma((memb,)),
+            dma((memb // 2,)), dma((memb // 2,)),
+            dma((memb // 2,)), dma((memb // 2,)), dma((2,)),
         ],
         compiler_params=pltpu.CompilerParams(
             collective_id=0, has_side_effects=True,
             vmem_limit_bytes=rows * cols * 4 + (16 << 20)),
-    )(support, clouds, member_weights)
+    )(support.T, clouds.swapaxes(1, 2), member_weights)
+    return out.T
 
 
 def solution(mesh):

time: 39.5 us -> 42.8 us (1.084)
  Pallas kernels: 36.6 us -> 39.6 us
    pallas_call x1, Pallas kernels: 36.6 us -> 39.6 us  [per_device(): pl.pallas_call(functools.partial(kernel, dims), out_shape=jax.ShapeDtypeS...]
    unnamed x4 -> x7, local copies, waits for them, and re-layouts: 1.92 us -> 2.89 us
    pallas_call x1 -> x0, local copies, waits for them, and re-layouts: 0.7 us -> none  [per_device(): pl.pallas_call(functools.partial(kernel, dims), out_shape=jax.ShapeDtypeS...]
where the time goes in v2:
time: 42.8 us; the launch traced here: 42.5 us
  Pallas kernels  39.6 us (93%)
  local copies, waits for them, and re-layouts  2.89 us (7%)
    pallas_call x1, Pallas kernels, per_device(): pl.pallas_call(functools.partial(kernel, dims), out_shape=jax.ShapeDtypeS...  39.6 us
    unnamed x7, local copies, waits for them, and re-layouts  2.89 us

profile of v2, /device:TPU:0, one launch (start us, length us, event | category | flops | bytes accessed | tf_op | source)
XLA Modules:
  0.0 42.5 jit_solution(14053983222103819135)
XLA Ops:
  0.0 0.0 copy-start.2
  0.0 0.7 %copy-done.2 = f32[8]{0:T(128)S(1)} copy-done((f32[8]{0:T(128)S(1)}, f32[8]{0:T(128)}, u32[]{:S(2)}) %copy-start.2) | copy-done | bytes 56
  0.7 0.0 copy-start
  0.7 0.9 %copy-done = bf16[8,128,64]{1,2,0:T(8,128)(2,1)S(1)} copy-done((bf16[8,128,64]{1,2,0:T(8,128)(2,1)S(1)}, bf16[8,128,64]{1,2,0:T(8,128)(2,1)}, u32[]{:S(2)}) %copy-start) | copy-done | bytes 131096
  1.6 0.0 copy-start.1
  1.6 0.7 %copy-done.1 = bf16[128,64]{0,1:T(8,128)(2,1)S(1)} copy-done((bf16[128,64]{0,1:T(8,128)(2,1)S(1)}, bf16[128,64]{0,1:T(8,128)(2,1)}, u32[]{:S(2)}) %copy-start.1) | copy-done | bytes 16408
  2.3 39.6 %shard_map.37 = f32[64,128]{1,0:T(8,128)S(1)} custom-call(bf16[64,128]{1,0:T(8,128)(2,1)S(1)} %bitcast.5, bf16[8,64,128]{2,1,0:T(8,128)(2,1)S(1)} %bitcast.3, f32[8]{0:T(128)S(1)} %copy-done.2), custom_call_target="tpu_custom_call" | custom-call | tf_op jit(solution)/shard_map/pallas_call | solution.py:347
  41.9 0.6 %copy.5 = f32[128,64]{0,1:T(8,128)} copy(f32[128,64]{0,1:T(8,128)S(1)} %bitcast.4) | data formatting | bytes 65536
Async XLA Ops:
  0.0 0.7 %copy-start.2 = (f32[8]{0:T(128)S(1)}, f32[8]{0:T(128)}, u32[]{:S(2)}) copy-start(f32[8]{0:T(128)} %weights_ref.1) | copy-start | bytes 100
  0.7 0.9 %copy-start = (bf16[8,128,64]{1,2,0:T(8,128)(2,1)S(1)}, bf16[8,128,64]{1,2,0:T(8,128)(2,1)}, u32[]{:S(2)}) copy-start(bf16[8,128,64]{1,2,0:T(8,128)(2,1)} %param.4) | copy-start | bytes 393220
  1.6 0.7 %copy-start.1 = (bf16[128,64]{0,1:T(8,128)(2,1)S(1)}, bf16[128,64]{0,1:T(8,128)(2,1)}, u32[]{:S(2)}) copy-start(bf16[128,64]{0,1:T(8,128)(2,1)} %param.3) | copy-start | bytes 49156

commit v3 on v1

--- a/solution.py
+++ b/solution.py
@@ -11,7 +11,7 @@
 ITERS = 3
 EPS = 0.05
 LANES = 128
-GROUP = 32
+GROUP = 64
 EXTRA = 16
 F32 = jnp.float32
 BF16 = jnp.bfloat16
@@ -25,10 +25,10 @@
 
 def kernel(
     dims, sup_ref, clouds_ref, weights_ref, out_ref,
-    sup_send, cloud_send, sup_buf, cloud_buf, left, right, mat, top, u_ref, part,
+    cloud_send, sup_buf, cloud_buf, left, right, mat, top, u_ref, part,
     col, stat_send, stat_recv, plan, out_send, out_recv,
     sup_ssem, sup_rsem, cl_ssem, cl_rsem, relay_ssem, relay_rsem,
-    stat_ssem, stat_rsem, out_ssem, out_rsem,
+    stat_ssem, stat_rsem, out_ssem, out_rsem, own_sem,
 ):
     memb, sib, shard, dim = dims
     devices = memb * sib
@@ -52,11 +52,15 @@
     for s in range(1, sib):
         pl.semaphore_signal(barrier, inc=1, device_id=at(mine, lax.rem(r + s, sib)))
 
-    sup_send[...] = jnp.transpose(sup_ref[...].astype(F32)).astype(BF16)
-    for k in range(memb):
-        cloud_send[k] = jnp.transpose(clouds_ref[k].astype(F32)).astype(BF16)
-    sup_buf[mine] = sup_send[...]
-    cloud_buf[me] = cloud_send[mine]
+    own_sup = pltpu.make_async_copy(sup_ref, sup_buf.at[mine], own_sem.at[0])
+    own_cloud = pltpu.make_async_copy(clouds_ref.at[mine], cloud_buf.at[me], own_sem.at[1])
+    staged = pltpu.make_async_copy(clouds_ref, cloud_send, own_sem.at[2])
+    staged.start()
+    own_sup.start()
+    own_cloud.start()
+    own_sup.wait()
+    own_cloud.wait()
+    staged.wait()
     pl.semaphore_wait(barrier, memb - 1 + sib - 1)
 
     def cloud_copy(d):
@@ -67,7 +71,7 @@
 
     def sup_copy(d):
         return pltpu.make_async_remote_copy(
-            sup_send, sup_buf.at[mine], sup_ssem.at[d], sup_rsem.at[d],
+            sup_buf.at[mine], sup_buf.at[mine], sup_ssem.at[d], sup_rsem.at[d],
             device_id=at(peer(d), r), device_id_type=pl.DeviceIdType.MESH)
 
     def relay_copy(d, s):
@@ -81,15 +85,11 @@
         if d not in order:
             order.append(d)
     for d in order:
+        sup_copy(d).start()
+    for d in order:
         cloud_copy(d).start()
-    for d in order:
-        sup_copy(d).start()
     for s in range(1, sib):
         relay_copy(0, s).start()
-    for d in range(1, memb):
-        cloud_copy(d).wait_recv()
-        for s in range(1, sib):
-            relay_copy(d, s).start()
 
     ones3 = jnp.ones((3, shard), F32)
     zeros = jnp.zeros((EXTRA - 6, shard), F32)
@@ -110,11 +110,15 @@
 
     for d in range(1, memb):
         sup_copy(d).wait_recv()
-    lax.fori_loop(0, memb, make_left, 0)
+    lax.fori_loop(0, memb, make_left, 0, unroll=2)
+    for d in range(1, memb):
+        cloud_copy(d).wait_recv()
+        for s in range(1, sib):
+            relay_copy(d, s).start()
     for d in range(memb):
         for s in range(1, sib):
             relay_copy(d, s).wait_recv()
-    lax.fori_loop(0, devices, make_right, 0)
+    lax.fori_loop(0, devices, make_right, 0, unroll=4)
 
     wide = 256
     def cost_step(j, _):
@@ -160,7 +164,7 @@
                 for c in range(tiles))
 
         start = tuple(jnp.full((8, LANES), -3e38, F32) for _ in range(tiles))
-        best = lax.fori_loop(0, groups, max_step, start)
+        best = lax.fori_loop(0, groups, max_step, start, unroll=2)
         for c in range(tiles):
             b = jnp.max(best[c], axis=0, keepdims=True)
             stat_send[0, :, base + c * LANES:base + (c + 1) * LANES] = b
@@ -196,7 +200,7 @@
                 part[pl.ds(pl.multiple_of(g * GROUP, GROUP), GROUP), :] = acc
                 return 0
 
-            lax.fori_loop(0, groups, row_step, 0)
+            lax.fori_loop(0, groups, row_step, 0, unroll=2)
         total = jnp.sum(part[...], axis=1, keepdims=True)
         u_ref[...] = jnp.broadcast_to(1.0 / (total * rows_all(dims)), u_ref.shape)
         for base in range(0, cols, chunk):
@@ -206,7 +210,7 @@
                     acc[c] + fold(mat[tile(g, base, c)] * u, jnp.add) for c in range(tiles))
 
             start = tuple(jnp.zeros((8, LANES), F32) for _ in range(tiles))
-            acc = lax.fori_loop(0, groups, col_step, start)
+            acc = lax.fori_loop(0, groups, col_step, start, unroll=2)
             for c in range(tiles):
                 stat_send[1 + step, :, base + c * LANES:base + (c + 1) * LANES] = jnp.sum(
                     acc[c], axis=0, keepdims=True)
@@ -263,7 +267,7 @@
     total = out_recv[0]
     for k in range(1, memb):
         total = total + out_recv[k]
-    out_ref[...] = jnp.transpose(total)
+    out_ref[...] = total
 
     for d in range(1, memb):
         cloud_copy(d).wait_send()
@@ -288,17 +292,16 @@
     rows, cols = memb * shard, devices * shard
     dims = (memb, sib, shard, dim)
     vmem, dma = pltpu.VMEM, pltpu.SemaphoreType.DMA
-    return pl.pallas_call(
+    out = pl.pallas_call(
         functools.partial(kernel, dims),
-        out_shape=jax.ShapeDtypeStruct((shard, dim), F32),
+        out_shape=jax.ShapeDtypeStruct((dim, shard), F32),
         in_specs=[
-            pl.BlockSpec(memory_space=pltpu.VMEM),
-            pl.BlockSpec(memory_space=pltpu.VMEM),
+            pl.BlockSpec(memory_space=pl.ANY),
+            pl.BlockSpec(memory_space=pl.ANY),
             pl.BlockSpec(memory_space=pltpu.SMEM),
         ],
         out_specs=pl.BlockSpec(memory_space=pltpu.VMEM),
         scratch_shapes=[
-            vmem((dim, shard), BF16),
             vmem((memb, dim, shard), BF16),
             vmem((memb, dim, shard), BF16),
             vmem((devices, dim, shard), BF16),
@@ -318,12 +321,13 @@
             dma((memb,)), dma((memb,)),
             dma((memb, sib)), dma((memb, sib)),
             dma((ITERS, sib)), dma((ITERS, sib)),
-            dma((memb,)), dma((memb,)),
+            dma((memb,)), dma((memb,)), dma((3,)),
         ],
         compiler_params=pltpu.CompilerParams(
             collective_id=0, has_side_effects=True,
             vmem_limit_bytes=rows * cols * 4 + (16 << 20)),
-    )(support, clouds, member_weights)
+    )(support.T, clouds.swapaxes(1, 2), member_weights)
+    return out.T
 
 
 def solution(mesh):

time: 39.5 us -> 37.7 us (0.954)
  Pallas kernels: 36.6 us -> 34.5 us
    pallas_call x1, Pallas kernels: 36.6 us -> 34.5 us  [per_device(): pl.pallas_call(functools.partial(kernel, dims), out_shape=jax.ShapeDtypeS...]
    unnamed x4 -> x7, local copies, waits for them, and re-layouts: 1.92 us -> 2.89 us
    pallas_call x1 -> x0, local copies, waits for them, and re-layouts: 0.7 us -> none  [per_device(): pl.pallas_call(functools.partial(kernel, dims), out_shape=jax.ShapeDtypeS...]
where the time goes in v3:
time: 37.7 us; the launch traced here: 37.4 us
  Pallas kernels  34.5 us (92%)
  local copies, waits for them, and re-layouts  2.89 us (8%)
    pallas_call x1, Pallas kernels, per_device(): pl.pallas_call(functools.partial(kernel, dims), out_shape=jax.ShapeDtypeS...  34.5 us
    unnamed x7, local copies, waits for them, and re-layouts  2.89 us

profile of v3, /device:TPU:0, one launch (start us, length us, event | category | flops | bytes accessed | tf_op | source)
XLA Modules:
  0.0 37.4 jit_solution(2386608837870829482)
XLA Ops:
  0.0 0.0 copy-start.2
  0.0 0.7 %copy-done.2 = f32[8]{0:T(128)S(1)} copy-done((f32[8]{0:T(128)S(1)}, f32[8]{0:T(128)}, u32[]{:S(2)}) %copy-start.2) | copy-done | bytes 56
  0.7 0.0 copy-start
  0.7 0.9 %copy-done = bf16[8,128,64]{1,2,0:T(8,128)(2,1)S(1)} copy-done((bf16[8,128,64]{1,2,0:T(8,128)(2,1)S(1)}, bf16[8,128,64]{1,2,0:T(8,128)(2,1)}, u32[]{:S(2)}) %copy-start) | copy-done | bytes 131096
  1.6 0.0 copy-start.1
  1.6 0.7 %copy-done.1 = bf16[128,64]{0,1:T(8,128)(2,1)S(1)} copy-done((bf16[128,64]{0,1:T(8,128)(2,1)S(1)}, bf16[128,64]{0,1:T(8,128)(2,1)}, u32[]{:S(2)}) %copy-start.1) | copy-done | bytes 16408
  2.3 34.5 %shard_map.37 = f32[64,128]{1,0:T(8,128)S(1)} custom-call(bf16[64,128]{1,0:T(8,128)(2,1)S(1)} %bitcast.5, bf16[8,64,128]{2,1,0:T(8,128)(2,1)S(1)} %bitcast.3, f32[8]{0:T(128)S(1)} %copy-done.2), custom_call_target="tpu_custom_call" | custom-call | tf_op jit(solution)/shard_map/pallas_call | solution.py:295
  36.8 0.6 %copy.5 = f32[128,64]{0,1:T(8,128)} copy(f32[128,64]{0,1:T(8,128)S(1)} %bitcast.4) | data formatting | bytes 65536
Async XLA Ops:
  0.0 0.7 %copy-start.2 = (f32[8]{0:T(128)S(1)}, f32[8]{0:T(128)}, u32[]{:S(2)}) copy-start(f32[8]{0:T(128)} %weights_ref.1) | copy-start | bytes 100
  0.7 0.9 %copy-start = (bf16[8,128,64]{1,2,0:T(8,128)(2,1)S(1)}, bf16[8,128,64]{1,2,0:T(8,128)(2,1)}, u32[]{:S(2)}) copy-start(bf16[8,128,64]{1,2,0:T(8,128)(2,1)} %param.4) | copy-start | bytes 393220
  1.6 0.7 %copy-start.1 = (bf16[128,64]{0,1:T(8,128)(2,1)S(1)}, bf16[128,64]{0,1:T(8,128)(2,1)}, u32[]{:S(2)}) copy-start(bf16[128,64]{0,1:T(8,128)(2,1)} %param.3) | copy-start | bytes 49156

commit v4 on v3

--- a/solution.py
+++ b/solution.py
@@ -110,7 +110,7 @@
 
     for d in range(1, memb):
         sup_copy(d).wait_recv()
-    lax.fori_loop(0, memb, make_left, 0, unroll=2)
+    lax.fori_loop(0, memb, make_left, 0, unroll=4)
     for d in range(1, memb):
         cloud_copy(d).wait_recv()
         for s in range(1, sib):
@@ -132,7 +132,7 @@
         return 0
 
     top[...] = jnp.full(top.shape, -3e38, F32)
-    lax.fori_loop(0, cols // wide, cost_step, 0)
+    lax.fori_loop(0, cols // wide, cost_step, 0, unroll=2)
     top[...] = jnp.broadcast_to(jnp.max(top[...], axis=1, keepdims=True), top.shape)
 
     tiles = chunk // LANES

time: 37.7 us -> 37.2 us (0.987)
  Pallas kernels: 34.5 us -> 34.1 us
    pallas_call x1, Pallas kernels: 34.5 us -> 34.1 us  [per_device(): pl.pallas_call(functools.partial(kernel, dims), out_shape=jax.ShapeDtypeS...]
where the time goes in v4:
time: 37.2 us; the launch traced here: 37 us
  Pallas kernels  34.1 us (92%)
  local copies, waits for them, and re-layouts  2.89 us (8%)
    pallas_call x1, Pallas kernels, per_device(): pl.pallas_call(functools.partial(kernel, dims), out_shape=jax.ShapeDtypeS...  34.1 us
    unnamed x7, local copies, waits for them, and re-layouts  2.89 us

profile of v4, /device:TPU:0, one launch (start us, length us, event | category | flops | bytes accessed | tf_op | source)
XLA Modules:
  0.0 37.0 jit_solution(17987727716884059897)
XLA Ops:
  0.0 0.0 copy-start.2
  0.0 0.7 %copy-done.2 = f32[8]{0:T(128)S(1)} copy-done((f32[8]{0:T(128)S(1)}, f32[8]{0:T(128)}, u32[]{:S(2)}) %copy-start.2) | copy-done | bytes 56
  0.7 0.0 copy-start
  0.7 0.9 %copy-done = bf16[8,128,64]{1,2,0:T(8,128)(2,1)S(1)} copy-done((bf16[8,128,64]{1,2,0:T(8,128)(2,1)S(1)}, bf16[8,128,64]{1,2,0:T(8,128)(2,1)}, u32[]{:S(2)}) %copy-start) | copy-done | bytes 131096
  1.6 0.0 copy-start.1
  1.6 0.7 %copy-done.1 = bf16[128,64]{0,1:T(8,128)(2,1)S(1)} copy-done((bf16[128,64]{0,1:T(8,128)(2,1)S(1)}, bf16[128,64]{0,1:T(8,128)(2,1)}, u32[]{:S(2)}) %copy-start.1) | copy-done | bytes 16408
  2.3 34.1 %shard_map.37 = f32[64,128]{1,0:T(8,128)S(1)} custom-call(bf16[64,128]{1,0:T(8,128)(2,1)S(1)} %bitcast.5, bf16[8,64,128]{2,1,0:T(8,128)(2,1)S(1)} %bitcast.3, f32[8]{0:T(128)S(1)} %copy-done.2), custom_call_target="tpu_custom_call" | custom-call | tf_op jit(solution)/shard_map/pallas_call | solution.py:295
  36.4 0.6 %copy.5 = f32[128,64]{0,1:T(8,128)} copy(f32[128,64]{0,1:T(8,128)S(1)} %bitcast.4) | data formatting | bytes 65536
Async XLA Ops:
  0.0 0.7 %copy-start.2 = (f32[8]{0:T(128)S(1)}, f32[8]{0:T(128)}, u32[]{:S(2)}) copy-start(f32[8]{0:T(128)} %weights_ref.1) | copy-start | bytes 100
  0.7 0.9 %copy-start = (bf16[8,128,64]{1,2,0:T(8,128)(2,1)S(1)}, bf16[8,128,64]{1,2,0:T(8,128)(2,1)}, u32[]{:S(2)}) copy-start(bf16[8,128,64]{1,2,0:T(8,128)(2,1)} %param.4) | copy-start | bytes 393220
  1.6 0.7 %copy-start.1 = (bf16[128,64]{0,1:T(8,128)(2,1)S(1)}, bf16[128,64]{0,1:T(8,128)(2,1)}, u32[]{:S(2)}) copy-start(bf16[128,64]{0,1:T(8,128)(2,1)} %param.3) | copy-start | bytes 49156
